TPU v7x, 512 devices: a whole 4x8x8 slice. The times are simulated.
512 devices in a mesh: row: 32 (over z, y_hi, core), col: 16 (over x, y_lo).
Axes of the slice: x: 4, y: 8 (y_hi: 2, y_lo: 4; y = y_hi * 4 + y_lo), z: 8, core: 2. Of those that a mesh axis runs over, the one named last changes fastest.
Arguments:
- rhs_top: bfloat16 [2, 1024, 16384], P(None, 'row', 'col'), may hold values from -6 to 6
- diag_inverse: bfloat16 [2, 1024, 1024], P(None, 'row'), as said below
- panel_coupling: bfloat16 [1024, 1024], P('row'), may hold values from -0.1875 to 0.1875
- trailing_factor: bfloat16 [32768, 2048], P('row', 'col'), may hold values from -0.125 to 0.125
- rhs_trailing: bfloat16 [32768, 16384], P('row', 'col'), may hold values from -6 to 6
Outputs:
- solved: bfloat16 [2, 1024, 16384], P(None, 'row', 'col')
- updated: bfloat16 [32768, 16384], P('row', 'col')
Inputs may be any that keep to these rules, and one draw needn't show every extreme that they name: Each diag_inverse[k] is lower triangular.
All inputs are finite; a program needn't handle non-finite values.
Results may differ from a plain program's by a relative error of at most 0.0055.
Values may be sent and summed in bfloat16 or wider, within the bound.
A program may use at most 64 MiB of HBM per device.

v0:
```python
import jax
import jax.numpy as jnp
from jax import lax
from jax.sharding import PartitionSpec as P


def fold_rows(inverse_rows, piece):
    return jnp.dot(inverse_rows, piece, preferred_element_type=jnp.float32)


def shards(rhs_top, diag_inverse, panel_coupling, trailing_factor, rhs_trailing):
    inverse_first = diag_inverse[0]
    inverse_second = diag_inverse[1]
    first_mine = fold_rows(
        inverse_first, lax.all_gather(rhs_top[0], "row", axis=0, tiled=True)
    ).astype(jnp.bfloat16)
    first_all = lax.all_gather(first_mine, "row", axis=0, tiled=True)
    carried = (
        rhs_top[1].astype(jnp.float32)
        - jnp.dot(panel_coupling, first_all, preferred_element_type=jnp.float32)
    ).astype(jnp.bfloat16)
    second_mine = fold_rows(
        inverse_second, lax.all_gather(carried, "row", axis=0, tiled=True)
    ).astype(jnp.bfloat16)
    second_all = lax.all_gather(second_mine, "row", axis=0, tiled=True)
    solution = jnp.concatenate([first_all, second_all], axis=0)
    total = jnp.dot(
        lax.all_gather(trailing_factor, "col", axis=1, tiled=True),
        solution,
        preferred_element_type=jnp.float32,
    )
    updated = (rhs_trailing.astype(jnp.float32) - total).astype(jnp.bfloat16)
    solved = jnp.stack([first_mine, second_mine])
    return (solved, updated)


def solution(mesh):
    in_specs = (
        P(None, "row", "col"),
        P(None, "row", None),
        P("row", None),
        P("row", "col"),
        P("row", "col"),
    )
    out_specs = (P(None, "row", "col"), P("row", "col"))
    return jax.shard_map(shards, mesh=mesh, in_specs=in_specs, out_specs=out_specs, check_vma=False)
```

profile of v0, /device:TPU:9, one launch (start us, length us, event | category | flops | bytes accessed | tf_op | source)
XLA Modules:
  0.0 514.1 jit_solution(12273619999213910419)
XLA Ops:
  7.2 0.0 copy-start
  7.2 0.0 all-gather.15.cloned.1.call-start
  7.2 1.5 slice.13
  8.7 0.0 all-gather.15.cloned.1.call-update
  8.8 0.0 all-gather.7.cloned.1.call-start
  8.8 101.2 %all-gather.15.cloned.1.call-done = bf16[1,1024,1024]{2,1,0:T(8,128)(2,1)} async-done(((bf16[1,32,1024]{2,1,0:T(8,128)(2,1)}), bf16[1,1024,1024]{2,1,0:T(8,128)(2,1)}) %all-gather.15.cloned.1.call-update) | async-done | bytes 2097168 | tf_op jit(solution)/shard_map/all_gather | solution.py:15
  110.0 2.7 fusion.11
  112.7 0.0 all-gather.7.cloned.1.call-update
  112.8 0.0 all-gather.9.cloned.1.call-start
  112.8 88.3 %all-gather.7.cloned.1.call-done = bf16[1024,1024]{1,0:T(8,128)(2,1)} async-done(((bf16[32,1024]{1,0:T(8,128)(2,1)}), bf16[1024,1024]{1,0:T(8,128)(2,1)}) %all-gather.7.cloned.1.call-update) | async-done | bytes 2097168 | tf_op jit(solution)/shard_map/all_gather | solution.py:17
  201.2 2.7 fusion.10
  203.9 0.0 all-gather.9.cloned.1.call-update
  203.9 0.0 all-gather.13.cloned.1.call-start
  203.9 0.5 all-gather.13.cloned.1.call-update
  204.5 0.0 all-gather.11.cloned.1.call-start
  204.5 87.8 %all-gather.9.cloned.1.call-done = bf16[1024,1024]{1,0:T(8,128)(2,1)} async-done(((bf16[32,1024]{1,0:T(8,128)(2,1)}), bf16[1024,1024]{1,0:T(8,128)(2,1)}) %all-gather.9.cloned.1.call-update) | async-done | bytes 2097168 | tf_op jit(solution)/shard_map/all_gather | solution.py:23
  292.3 2.7 convolution_convert_fusion
  295.0 0.0 all-gather.11.cloned.1.call-update
  295.1 2.6 copy.7
  297.6 0.7 pad_maximum_fusion
  298.3 98.5 %all-gather.13.cloned.1.call-done = bf16[1024,2048]{1,0:T(8,128)(2,1)} async-done(((bf16[1024,128]{1,0:T(8,128)(2,1)}), bf16[1024,2048]{1,0:T(8,128)(2,1)}) %all-gather.13.cloned.1.call-update) | async-done | bytes 4194320 | tf_op jit(solution)/shard_map/all_gather | solution.py:28
  396.8 99.6 %all-gather.11.cloned.1.call-done = bf16[1024,1024]{1,0:T(8,128)(2,1)} async-done(((bf16[32,1024]{1,0:T(8,128)(2,1)}), bf16[1024,1024]{1,0:T(8,128)(2,1)}) %all-gather.11.cloned.1.call-update) | async-done | bytes 2097168 | tf_op jit(solution)/shard_map/all_gather | solution.py:25
  496.4 8.6 %fusion.4 = bf16[1024,1024]{0,1:T(8,128)(2,1)S(1)} fusion(bf16[1024,1024]{0,1:T(8,128)(2,1)} %copy.7, bf16[1024,2048]{1,0:T(8,128)(2,1)} %all-gather.13.cloned.1.call-done, bf16[1024,1024]{1,0:T(8,128)(2,1)} %all-gather.11.cloned.1.call-done, bf16[1024,1024]{1,0:T(8,128)(2,1)} %all-gather.7.cloned.1.call-done), kind=kOutput, calls=%fused_computation.5 | convolution fusion | flops 4306501632 | bytes 12582912 | tf_op jit(solution)/shard_map/dot_general | solution.py:27
  505.0 2.6 copy.8
  (11 shorter events, 0.0 us)
Async XLA Ops:
  7.2 194.0 %copy-start = (bf16[32,1024]{1,0:T(8,128)(2,1)S(1)}, bf16[32,1024]{1,0:T(8,128)(2,1)}, u32[]{:S(2)}) copy-start(bf16[32,1024]{1,0:T(8,128)(2,1)} %param.7) | copy-start | bytes 196612
  7.2 194.0 %copy-start.5 = (bf16[2,32,1024]{2,1,0:T(8,128)(2,1)S(1)}, bf16[2,32,1024]{2,1,0:T(8,128)(2,1)}, u32[]{:S(2)}) copy-start(bf16[2,32,1024]{2,1,0:T(8,128)(2,1)} %param.5) | copy-start | bytes 393220
  7.2 102.8 %all-gather.15.cloned.1.call-start = ((), (), s32[]{:S(2)}) async-start(), calls=%async_computation.4 | async-start | bytes 2162688 | tf_op jit(solution)/shard_map/all_gather | solution.py:15
  8.8 283.6 %copy-start.4 = (bf16[2,32,1024]{2,1,0:T(8,128)(2,1)S(1)}, bf16[2,32,1024]{2,1,0:T(8,128)(2,1)}, u32[]{:S(2)}) copy-start(bf16[2,32,1024]{2,1,0:T(8,128)(2,1)} %param.6) | copy-start | bytes 393220
  8.8 192.4 %all-gather.7.cloned.1.call-start = ((), (), s32[]{:S(2)}) async-start(), calls=%async_computation | async-start | bytes 2162688 | tf_op jit(solution)/shard_map/all_gather | solution.py:17
  112.8 182.3 %copy-start.1 = (bf16[1024,1024]{1,0:T(8,128)(2,1)S(1)}, bf16[1024,1024]{1,0:T(8,128)(2,1)}, u32[]{:S(2)}) copy-start(bf16[1024,1024]{1,0:T(8,128)(2,1)} %param.9) | copy-start | bytes 6291460
  112.8 179.5 %all-gather.9.cloned.1.call-start = ((), (), s32[]{:S(2)}) async-start(), calls=%async_computation.1 | async-start | bytes 2162688 | tf_op jit(solution)/shard_map/all_gather | solution.py:23
  203.9 192.9 %all-gather.13.cloned.1.call-start = ((), (), s32[]{:S(2)}) async-start(), calls=%async_computation.3 | async-start | bytes 4456448 | tf_op jit(solution)/shard_map/all_gather | solution.py:28
  204.5 292.0 %all-gather.11.cloned.1.call-start = ((), (), s32[]{:S(2)}) async-start(), calls=%async_computation.2 | async-start | bytes 2162688 | tf_op jit(solution)/shard_map/all_gather | solution.py:25
  295.0 2.6 copy-start.2
  295.1 2.6 copy-start.3
Sparse Core Ops, SparseCore 0:
  12.0 97.9 all-gather.14
  114.0 87.1 all-gather.6
  205.1 87.1 all-gather.8
  294.2 102.5 all-gather.12
  400.0 96.3 all-gather.10
where the time goes:
time: 514 us
  waiting for transfers between devices  476 us (93%)
  matrix products  16.7 us (3%)
  between operations  13.8 us (3%)
  local copies, waits for them, and re-layouts  6.67 us (1%)
    all_gather x1, waiting for transfers between devices, shards(): lax.all_gather(rhs_top[0], 'row', axis=0, tiled=True)  101 us
    all_gather x1, waiting for transfers between devices, shards(): second_all = lax.all_gather(second_mine, 'row', axis=0, tiled=True)  99.6 us
    all_gather x1, waiting for transfers between devices, shards(): lax.all_gather(trailing_factor, 'col', axis=1, tiled=True)  98.5 us
    all_gather x1, waiting for transfers between devices, shards(): first_all = lax.all_gather(first_mine, 'row', axis=0, tiled=True)  88.3 us
    all_gather x1, waiting for transfers between devices, shards(): lax.all_gather(carried, 'row', axis=0, tiled=True)  87.8 us
  transfers between devices with their start and end apart: 5, of which 5 were waited for; matrix products, arithmetic and copies ran while one was open for 1% of the time, Pallas kernels for 0%

commit v1 on v0

--- a/solution.py
+++ b/solution.py
@@ -2,6 +2,17 @@
 import jax.numpy as jnp
 from jax import lax
 from jax.sharding import PartitionSpec as P
+from jax.lax import all_to_all, axis_size
+
+
+def _point_core(field_in):
+    taken_in = jnp.concatenate(
+        all_to_all(
+            jnp.stack(axis_size("row") * [field_in], axis=0), "row", split_axis=0, concat_axis=0
+        ),
+        axis=0,
+    )
+    return taken_in
 
 
 def fold_rows(inverse_rows, piece):
@@ -14,7 +25,7 @@
     first_mine = fold_rows(
         inverse_first, lax.all_gather(rhs_top[0], "row", axis=0, tiled=True)
     ).astype(jnp.bfloat16)
-    first_all = lax.all_gather(first_mine, "row", axis=0, tiled=True)
+    first_all = _point_core(first_mine)
     carried = (
         rhs_top[1].astype(jnp.float32)
         - jnp.dot(panel_coupling, first_all, preferred_element_type=jnp.float32)

time: 514 us -> 488 us (0.949)
  waiting for transfers between devices: 476 us -> 388 us
  blocking collectives: 0 us -> 59.8 us
    all_gather x1 -> x0, waiting for transfers between devices: 88.3 us -> none  [shards(): first_all = lax.all_gather(first_mine, 'row', axis=0, tiled=True)]
    all_to_all x0 -> x1, blocking collectives: none -> 59.8 us  [_point_core(): all_to_all(jnp.stack(axis_size('row') * [field_in], axis=0), 'row', split...]
  transfers between devices with their start and end apart: 5 -> 4, of which waited for: 5 -> 4; matrix products, arithmetic and copies ran while one was open for 1% -> 2% of each run, Pallas kernels for 0% -> 0%
where the time goes in v1:
time: 488 us; the launch traced here: 487 us
  waiting for transfers between devices  388 us (80%)
  blocking collectives  59.8 us (12%)
  matrix products  15.2 us (3%)
  between operations  13.8 us (3%)
  local copies, waits for them, and re-layouts  9.66 us (2%)
    all_gather x1, waiting for transfers between devices, shards(): lax.all_gather(rhs_top[0], 'row', axis=0, tiled=True)  101 us
    all_gather x1, waiting for transfers between devices, shards(): second_all = lax.all_gather(second_mine, 'row', axis=0, tiled=True)  99.6 us
    all_gather x1, waiting for transfers between devices, shards(): lax.all_gather(trailing_factor, 'col', axis=1, tiled=True)  97.3 us
    all_gather x1, waiting for transfers between devices, shards(): lax.all_gather(carried, 'row', axis=0, tiled=True)  89.1 us
    all_to_all x1, blocking collectives, _point_core(): all_to_all(jnp.stack(axis_size('row') * [field_in], axis=0), 'row', split...  59.8 us
  transfers between devices with their start and end apart: 4, of which 4 were waited for; matrix products, arithmetic and copies ran while one was open for 2% of the time, Pallas kernels for 0%

profile of v1, /device:TPU:9, one launch (start us, length us, event | category | flops | bytes accessed | tf_op | source)
XLA Modules:
  0.0 487.2 jit_solution(7353547653526887593)
XLA Ops:
  7.2 0.0 copy-start
  7.2 0.0 all-gather.12.cloned.1.call-start
  7.2 1.5 slice.13
  8.7 0.0 all-gather.12.cloned.1.call-update
  8.7 0.0 all-gather.6.cloned.1.call-start
  8.8 101.2 %all-gather.12.cloned.1.call-done = bf16[1,1024,1024]{2,1,0:T(8,128)(2,1)} async-done(((bf16[1,32,1024]{2,1,0:T(8,128)(2,1)}), bf16[1,1024,1024]{2,1,0:T(8,128)(2,1)}) %all-gather.12.cloned.1.call-update) | async-done | bytes 2097168 | tf_op jit(solution)/shard_map/all_gather | solution.py:26
  110.0 2.1 fusion.11
  112.1 0.3 stack.9
  112.4 0.0 copy-start.3
  112.4 59.8 %all_to_all.5 = bf16[32,32,1024]{2,1,0:T(8,128)(2,1)S(1)} all-to-all(bf16[32,32,1024]{2,1,0:T(8,128)(2,1)S(1)} %stack.9), channel_id=1, replica_groups=mesh['row'=32,'col'=16] {'row'}, dimensions={0} | all-to-all | bytes 4194304 | tf_op jit(solution)/shard_map/all_to_all | solution.py:10
  172.1 1.1 fusion.10
  173.2 0.0 all-gather.6.cloned.1.call-update
  173.3 0.0 all-gather.10.cloned.1.call-start
  173.3 0.7 all-gather.10.cloned.1.call-update
  174.0 0.0 all-gather.8.cloned.1.call-start
  174.1 89.1 %all-gather.6.cloned.1.call-done = bf16[1024,1024]{1,0:T(8,128)(2,1)} async-done(((bf16[32,1024]{1,0:T(8,128)(2,1)}), bf16[1024,1024]{1,0:T(8,128)(2,1)}) %all-gather.6.cloned.1.call-update) | async-done | bytes 2097168 | tf_op jit(solution)/shard_map/all_gather | solution.py:34
  263.2 2.7 convolution_convert_fusion
  265.9 0.0 all-gather.8.cloned.1.call-update
  265.9 4.0 copy.7
  269.9 0.7 pad_maximum_fusion
  270.5 97.3 %all-gather.10.cloned.1.call-done = bf16[1024,2048]{1,0:T(8,128)(2,1)} async-done(((bf16[1024,128]{1,0:T(8,128)(2,1)}), bf16[1024,2048]{1,0:T(8,128)(2,1)}) %all-gather.10.cloned.1.call-update) | async-done | bytes 4194320 | tf_op jit(solution)/shard_map/all_gather | solution.py:39
  367.8 99.6 %all-gather.8.cloned.1.call-done = bf16[1024,1024]{1,0:T(8,128)(2,1)} async-done(((bf16[32,1024]{1,0:T(8,128)(2,1)}), bf16[1024,1024]{1,0:T(8,128)(2,1)}) %all-gather.8.cloned.1.call-update) | async-done | bytes 2097168 | tf_op jit(solution)/shard_map/all_gather | solution.py:36
  467.4 9.4 %fusion.4 = bf16[1024,1024]{0,1:T(8,128)(2,1)} fusion(bf16[1024,1024]{0,1:T(8,128)(2,1)} %copy.7, bf16[1024,2048]{1,0:T(8,128)(2,1)} %all-gather.10.cloned.1.call-done, bf16[1024,1024]{1,0:T(8,128)(2,1)} %all-gather.8.cloned.1.call-done, bf16[1024,1024]{1,0:T(8,128)(2,1)S(1)} %bitcast.34), kind=kOutput, calls=%fused_computation.5 | convolution fusion | flops 4306501632 | bytes 12582912 | tf_op jit(solution)/shard_map/dot_general | solution.py:38
  476.8 3.9 copy.8
  (6 shorter events, 0.0 us)
Async XLA Ops:
  7.2 165.0 %copy-start = (bf16[32,1024]{1,0:T(8,128)(2,1)S(1)}, bf16[32,1024]{1,0:T(8,128)(2,1)}, u32[]{:S(2)}) copy-start(bf16[32,1024]{1,0:T(8,128)(2,1)} %param.7) | copy-start | bytes 196612
  7.2 102.8 %all-gather.12.cloned.1.call-start = ((), (), s32[]{:S(2)}) async-start(), calls=%async_computation.4 | async-start | bytes 2162688 | tf_op jit(solution)/shard_map/all_gather | solution.py:26
  8.7 254.4 %all-gather.6.cloned.1.call-start = ((), (), s32[]{:S(2)}) async-start(), calls=%async_computation.1 | async-start | bytes 2162688 | tf_op jit(solution)/shard_map/all_gather | solution.py:34
  112.4 59.8 %copy-start.3 = (bf16[2,32,1024]{2,1,0:T(8,128)(2,1)S(1)}, bf16[2,32,1024]{2,1,0:T(8,128)(2,1)}, u32[]{:S(2)}) copy-start(bf16[2,32,1024]{2,1,0:T(8,128)(2,1)} %param.5) | copy-start | bytes 393220
  172.1 91.0 %copy-start.2 = (bf16[2,32,1024]{2,1,0:T(8,128)(2,1)S(1)}, bf16[2,32,1024]{2,1,0:T(8,128)(2,1)}, u32[]{:S(2)}) copy-start(bf16[2,32,1024]{2,1,0:T(8,128)(2,1)} %param.6) | copy-start | bytes 393220
  173.3 194.5 %all-gather.10.cloned.1.call-start = ((), (), s32[]{:S(2)}) async-start(), calls=%async_computation.3 | async-start | bytes 4456448 | tf_op jit(solution)/shard_map/all_gather | solution.py:39
  174.0 293.4 %all-gather.8.cloned.1.call-start = ((), (), s32[]{:S(2)}) async-start(), calls=%async_computation.2 | async-start | bytes 2162688 | tf_op jit(solution)/shard_map/all_gather | solution.py:36
  265.9 4.0 copy-start.1
Sparse Core Ops, SparseCore 0:
  12.0 97.9 all-gather.11
  173.4 89.7 all-gather.5
  265.2 102.5 all-gather.9
  371.0 96.3 all-gather.7
